TPU v7x, 32 devices: a whole 2x2x4 slice. The times are simulated.
32 devices in a mesh: pipe: 4 (over y, core), tensor: 4 (over z), dp: 2 (over x).
Axes of the slice: x: 2, y: 2, z: 4, core: 2. Of those that a mesh axis runs over, the one named last changes fastest.
Arguments:
- out_grad: bfloat16 [4, 2, 128, 2560], P('pipe', 'dp', None, 'tensor'), may hold values from -6 to 6
- gate_pre: bfloat16 [4, 2, 13824, 128], P('pipe', 'dp', 'tensor'), may hold values from -6 to 6
- up_pre: bfloat16 [4, 2, 13824, 128], P('pipe', 'dp', 'tensor'), may hold values from -6 to 6
- down_weight: bfloat16 [4, 13824, 2560], P('pipe', 'tensor'), may hold values from -0.125 to 0.125
Outputs:
- gate_grad: bfloat16 [4, 2, 13824, 128], P('pipe', 'dp', 'tensor')
- up_grad: bfloat16 [4, 2, 13824, 128], P('pipe', 'dp', 'tensor')
- weight_grad: bfloat16 [4, 13824, 2560], P('pipe', 'tensor', 'dp')
All inputs are finite; a program needn't handle non-finite values.
Results may differ from a plain program's by a relative error of at most 0.0075.
Values may be sent and summed in bfloat16 or wider, within the bound.
No kernel may reach another device: no remote copies, remote signals or barrier semaphores. Data moves between devices by JAX's collectives and lax.ppermute only.
A program may use at most 64 MiB of HBM per device.

v0:
```python
import functools

import jax
import jax.numpy as jnp
from jax import lax
from jax.experimental import pallas as pl
from jax.experimental.pallas import tpu as pltpu
from jax.sharding import PartitionSpec as P


BF16 = jnp.bfloat16
F32 = jnp.float32


def shifted(value, axis, step):
    size = lax.axis_size(axis)
    return lax.ppermute(value, axis, [(i, (i + step) % size) for i in range(size)])


def crossed(value, axis, mask):
    return lax.ppermute(value, axis, [(i, i ^ mask) for i in range(lax.axis_size(axis))])


def mirrored(value):
    return crossed(value, "pipe", lax.axis_size("pipe") // 2)


def opposite(value):
    n_pipe, n_dp = lax.axis_size("pipe"), lax.axis_size("dp")
    mask = n_pipe // 2 * n_dp + 1
    return lax.ppermute(
        value, ("pipe", "dp"), [(i, i ^ mask) for i in range(n_pipe * n_dp)]
    )


HIDDEN_LIMIT = 60 << 20
LOAD_LIMIT = 30 << 20
GRADS_LIMIT = 6 << 20


def hidden_kernel(cuts, gate_hbm, up_hbm, *refs):
    outs, (gate, up, sems) = refs[:-3], refs[-3:]
    copies = []
    for k, (start, count) in enumerate(cuts[2:]):
        part = pl.ds(start, count)
        pair = [
            pltpu.make_async_copy(gate_hbm.at[0, 0, part], gate.at[part], sems.at[0, k]),
            pltpu.make_async_copy(up_hbm.at[0, 0, part], up.at[part], sems.at[1, k]),
        ]
        for copy in pair:
            copy.start()
        copies.append(pair)
    for (start, count), pair, out in zip(cuts[2:], copies, outs[2:]):
        for copy in pair:
            copy.wait()
        g = gate[start : start + count].astype(F32)
        u = up[start : start + count].astype(F32)
        value = (g * jax.nn.sigmoid(g) * u).astype(BF16)
        out[...] = value
        for (first, size), whole in zip(cuts[:2], outs[:2]):
            if first <= start < first + size:
                whole[start - first : start - first + count] = value


def hidden_pieces(gate_pre, up_pre, cuts):
    rows, tokens = gate_pre.shape[2:]
    return pl.pallas_call(
        functools.partial(hidden_kernel, cuts),
        in_specs=[pl.BlockSpec(memory_space=pl.ANY)] * 2,
        out_specs=[pl.BlockSpec(memory_space=pltpu.VMEM)] * len(cuts),
        out_shape=[jax.ShapeDtypeStruct((count, tokens), BF16) for _, count in cuts],
        scratch_shapes=[
            pltpu.VMEM((rows, tokens), BF16),
            pltpu.VMEM((rows, tokens), BF16),
            pltpu.SemaphoreType.DMA((2, len(cuts))),
        ],
        compiler_params=pltpu.CompilerParams(vmem_limit_bytes=HIDDEN_LIMIT),
        cost_estimate=pl.CostEstimate(
            flops=16 * rows * tokens,
            bytes_accessed=6 * rows * tokens,
            transcendentals=2 * rows * tokens,
        ),
        name="hidden",
    )(gate_pre, up_pre)


def product(weight, grads):
    return lax.dot_general(weight, grads, (((1,), (1,)), ((), ())), preferred_element_type=F32)


def part_of(weight, rows, z, flips, shard):
    parts = [
        weight[rows, pl.ds(pl.multiple_of((z ^ flip) * shard, 128), shard)] for flip in flips
    ]
    return parts[0] if len(parts) == 1 else jnp.concatenate(parts, axis=1)


def load_kernel(tile, weight_hbm, own_hbm, weight, own, acc_ref, turned, w_sems, own_sem):
    tiles = weight.shape[0] // tile
    z = lax.axis_index("tensor")

    def weight_copy(k):
        rows = pl.ds(pl.multiple_of(k * tile, 16), tile)
        return pltpu.make_async_copy(weight_hbm.at[0, rows], weight.at[rows], w_sems.at[k])

    first = pltpu.make_async_copy(own_hbm.at[0, 0], own, own_sem)
    first.start()
    for k in range(4):
        weight_copy(k).start()
    first.wait()
    turned[...] = own[...].T

    @pl.loop(0, tiles)
    def _(k):
        weight_copy(k).wait()

        @pl.when(k + 4 < tiles)
        def _():
            weight_copy(k + 4).start()

        rows = pl.ds(pl.multiple_of(k * tile, 16), tile)
        acc_ref[rows] = jnp.dot(
            part_of(weight, rows, z, (0,), own.shape[1]),
            turned[...],
            preferred_element_type=F32,
        )


def load_all(weight, out_grad, tile):
    rows, width = weight.shape[1:]
    tokens, shard = out_grad.shape[2:]
    vmem, hbm = (pl.BlockSpec(memory_space=m) for m in (pltpu.VMEM, pl.ANY))
    return pl.pallas_call(
        functools.partial(load_kernel, tile),
        in_specs=[hbm] * 2,
        out_specs=[vmem] * 3,
        out_shape=[
            jax.ShapeDtypeStruct((rows, width), BF16),
            jax.ShapeDtypeStruct((tokens, shard), BF16),
            jax.ShapeDtypeStruct((rows, tokens), F32),
        ],
        scratch_shapes=[
            pltpu.VMEM((shard, tokens), BF16),
            pltpu.SemaphoreType.DMA((rows // tile,)),
            pltpu.SemaphoreType.DMA,
        ],
        compiler_params=pltpu.CompilerParams(vmem_limit_bytes=LOAD_LIMIT),
        cost_estimate=pl.CostEstimate(
            flops=2 * rows * shard * tokens, bytes_accessed=2 * rows * width, transcendentals=0
        ),
        name="load_all",
    )(weight, out_grad)


def grads_kernel(flips, tile, *refs):
    shards, weight, acc_ref, refs = refs[0], refs[1], refs[2], refs[3:]
    turned = refs[-1]
    shard = shards.shape[-1]
    step = pl.program_id(0)

    @pl.when(step == 0)
    def _():
        for k in range(len(flips)):
            turned[k * shard : (k + 1) * shard] = shards[k].T

    rows = pl.ds(pl.multiple_of(step * tile, 16), tile)
    z = lax.axis_index("tensor")
    hidden_grad = acc_ref[rows] + jnp.dot(
        part_of(weight, rows, z, flips, shard), turned[...], preferred_element_type=F32
    )
    if len(refs) == 2:
        refs[0][rows] = hidden_grad
        return
    gate, up, gg_ref, ug_ref = refs[:4]
    g = gate[0, 0, rows].astype(F32)
    u = up[0, 0, rows].astype(F32)
    sig = jax.nn.sigmoid(g)
    gg_ref[0, 0] = (hidden_grad * u * sig * (1.0 + g * (1.0 - sig))).astype(BF16)
    ug_ref[0, 0] = (hidden_grad * g * sig).astype(BF16)


def input_grads(shards, flips, tile, weight, acc, *inputs):
    rows = weight.shape[0]
    n, tokens, shard = shards.shape
    vmem = pl.BlockSpec(memory_space=pltpu.VMEM)
    if inputs:
        out_specs = [pl.BlockSpec((1, 1, tile, tokens), lambda i: (0, 0, i, 0))] * 2
        out_shape = [jax.ShapeDtypeStruct((1, 1, rows, tokens), BF16)] * 2
    else:
        out_specs, out_shape = vmem, jax.ShapeDtypeStruct((rows, tokens), F32)
    return pl.pallas_call(
        functools.partial(grads_kernel, flips, tile),
        grid=(rows // tile,),
        in_specs=[vmem] * (3 + len(inputs)),
        out_specs=out_specs,
        out_shape=out_shape,
        scratch_shapes=[pltpu.VMEM((n * shard, tokens), BF16)],
        compiler_params=pltpu.CompilerParams(vmem_limit_bytes=GRADS_LIMIT),
        cost_estimate=pl.CostEstimate(
            flops=2 * rows * n * shard * tokens,
            bytes_accessed=2 * rows * n * shard,
            transcendentals=0,
        ),
        name="input_grads",
    )(shards, weight, acc, *inputs)


def in_vmem(kernel, operands, shapes):
    vmem = pl.BlockSpec(memory_space=pltpu.VMEM)
    return pl.pallas_call(
        kernel,
        in_specs=[vmem] * len(operands),
        out_specs=[vmem] * len(shapes),
        out_shape=[jax.ShapeDtypeStruct(shape, BF16) for shape in shapes],
        compiler_params=pltpu.CompilerParams(vmem_limit_bytes=4 << 20),
    )(*operands)


def choose_kernel(own_ref, far_ref, mine_ref, theirs_ref, pair_ref):
    same = lax.axis_index("tensor") // 2 == lax.axis_index("dp")
    pair_ref[0] = own_ref[...]
    pair_ref[1] = far_ref[...]

    @pl.when(same)
    def _():
        mine_ref[...] = own_ref[...]
        theirs_ref[...] = far_ref[...]

    @pl.when(jnp.logical_not(same))
    def _():
        mine_ref[...] = far_ref[...]
        theirs_ref[...] = own_ref[...]


def stack_kernel(*refs):
    for k, ref in enumerate(refs[:-1]):
        refs[-1][k] = ref[...]


def cut_kernel(starts, *refs):
    n = len(starts)
    for k, ref in enumerate(refs[:2]):
        for start, out in zip(starts, refs[2 + k * n : 2 + (k + 1) * n]):
            out[...] = ref[start : start + out.shape[0]]


def weight_kernel(scale, starts, steps, tile, *refs):
    hid = refs[:8]
    mine, pair_other, g_other = refs[8:12], refs[12], refs[13]
    out_ref, cols_ref = refs[-2:]
    tokens, shard = mine[0].shape
    step = pl.program_id(0)

    @pl.when(step == 0)
    def _():
        z = lax.axis_index("tensor")
        half = lax.rem(z, 2)
        same = z // 2 == lax.axis_index("dp")

        def columns(place):
            return pl.ds(pl.multiple_of(place * shard, 128), shard)

        for k, ref in enumerate(mine):
            cols_ref[k * tokens : (k + 1) * tokens, columns(half)] = ref[...]
        cols_ref[:tokens, columns(1 - half)] = jnp.where(same, pair_other[0], pair_other[1])
        for k in range(3):
            cols_ref[(k + 1) * tokens : (k + 2) * tokens, columns(1 - half)] = g_other[k]

    for k in range(2):

        @pl.when((step >= k * steps) & (step < (k + 1) * steps))
        def _(k=k):
            at = (step - k * steps) * tile
            parts = [
                ref[pl.ds(pl.multiple_of(start + at, 16), tile)]
                for ref, start in zip(hid[4 * k : 4 * k + 4], starts[4 * k : 4 * k + 4])
            ]
            lhs = jnp.concatenate(parts, axis=1)
            total = jnp.dot(lhs, cols_ref[...], preferred_element_type=F32)
            out_ref[0] = (total * scale).astype(BF16)


def weight_rows(groups, rows, start, count, grads, scale, tile, previous=None):
    half = rows // 2
    tokens, shard = grads[0].shape
    steps = count // tile
    pairs = [pair for group in groups for pair in group]
    operands = [ref for ref, _ in pairs] + list(grads)
    in_specs = [pl.BlockSpec(memory_space=pltpu.VMEM)] * len(operands)
    aliases = {}
    if previous is not None:
        aliases = {len(operands): 0}
        in_specs.append(pl.BlockSpec(memory_space=pl.ANY))
        operands.append(previous)

    def place(i):
        return (0, i // steps * (half // tile) + start // tile + i % steps, 0)

    return pl.pallas_call(
        functools.partial(weight_kernel, scale, [first for _, first in pairs], steps, tile),
        grid=(2 * steps,),
        in_specs=in_specs,
        out_specs=pl.BlockSpec((1, tile, 2 * shard), place),
        out_shape=jax.ShapeDtypeStruct((1, rows, 2 * shard), BF16),
        input_output_aliases=aliases,
        scratch_shapes=[pltpu.VMEM((4 * tokens, 2 * shard), BF16)],
        compiler_params=pltpu.CompilerParams(vmem_limit_bytes=16 << 20),
        cost_estimate=pl.CostEstimate(
            flops=2 * 2 * count * 4 * tokens * 2 * shard,
            bytes_accessed=4 * count * (4 * tokens + 2 * shard),
            transcendentals=0,
        ),
        name="weight_rows",
    )(*operands)


def on_device_quad(out_grad, gate_pre, up_pre, down_weight):
    own = out_grad[0, 0]
    tokens, _ = own.shape
    rows = gate_pre.shape[2]
    half = rows // 2
    pieces = (0, half // 2, half)

    def to_x(value):
        return shifted(value, "dp", 1)

    def to_z(mask):
        return lambda value: crossed(value, "tensor", mask)

    n = len(pieces) - 1
    cuts = [(at + pieces[k], pieces[k + 1] - pieces[k]) for at in (0, half) for k in range(n)]
    hid = hidden_pieces(gate_pre, up_pre, ((0, half), (half, half), *cuts))
    hid_a, hid_b, hid = hid[0], hid[1], hid[2:]
    far = to_z(2)(own)
    a_y = mirrored(hid_a)
    b_x = to_x(hid_b)
    weight, own, acc = load_all(down_weight, out_grad, rows // 8)
    shapes = [own.shape] * 2 + [(2, *own.shape)]
    mine, theirs, pair = in_vmem(choose_kernel, (own, far), shapes)
    g_d = opposite(theirs)
    g_x = to_x(theirs)
    g_y = mirrored(mine)
    pair_other = to_z(1)(pair)
    acc = input_grads(far[None], (2,), rows // 4, weight, acc)
    stacked = in_vmem(stack_kernel, (g_y, g_x, g_d), [(3, *own.shape)])[0]
    g_other = to_z(1)(stacked)
    starts = pieces[:-1]
    shapes = [(end - start, tokens) for start, end in zip(starts, pieces[1:])]
    cuts = in_vmem(functools.partial(cut_kernel, starts), (a_y, b_x), shapes * 2)
    a_d = [to_x(cuts[k]) for k in range(n)]
    b_d = [mirrored(cuts[n + k]) for k in range(n)]
    a_x = [to_x(hid[k]) for k in range(n)]
    b_y = [mirrored(hid[n + k]) for k in range(n)]
    gate_grad, up_grad = input_grads(pair_other, (1, 3), rows // 8, weight, acc, gate_pre, up_pre)
    scale = 32.0 / (2.0 * 2 * tokens)
    out = None
    for k in range(n):
        first = pieces[k]
        a_parts = [(hid_a, first), (a_y, first), (a_x[k], 0), (a_d[k], 0)]
        b_parts = [(hid_b, first), (b_y[k], 0), (b_x, first), (b_d[k], 0)]
        out = weight_rows(
            [a_parts, b_parts],
            rows,
            first,
            pieces[k + 1] - first,
            [mine, g_y, g_x, g_d, pair_other, g_other],
            scale,
            half // 4,
            out,
        )
    return gate_grad, up_grad, out


def on_device(out_grad, gate_pre, up_pre, down_weight):
    n_dp = lax.axis_size("dp")
    n_tensor = lax.axis_size("tensor")
    own_grad = out_grad[0, 0]
    tokens, shard = own_grad.shape
    rows = gate_pre.shape[2]
    if n_dp == 2 and n_tensor == 4 and shard % 128 == 0 and rows % 384 == 0:
        return on_device_quad(out_grad, gate_pre, up_pre, down_weight)
    width = shard * n_tensor
    block = width // n_dp
    pieces = 3
    chunk = rows // pieces
    z = lax.axis_index("tensor")
    x = lax.axis_index("dp")

    grad_full = jnp.zeros((tokens, width), BF16)
    grad_full = lax.dynamic_update_slice(grad_full, own_grad, (0, z * shard))
    for step in range(1, n_tensor):
        got = shifted(own_grad, "tensor", step)
        grad_full = lax.dynamic_update_slice(
            grad_full, got, (0, (z - step) % n_tensor * shard)
        )

    gate = gate_pre[0, 0].astype(F32)
    up = up_pre[0, 0].astype(F32)
    sig = jax.nn.sigmoid(gate)
    hidden = (gate * sig * up).astype(BF16)
    hid = [hidden[i * chunk : (i + 1) * chunk] for i in range(pieces)]
    hid_y = [mirrored(h) for h in hid]
    hid_x = [[shifted(h, "dp", s) for h in hid] for s in range(1, n_dp)]
    hid_d = [
        [
            mirrored(hid_x[s - 1][i]) if i == pieces - 1 else shifted(hid_y[i], "dp", s)
            for i in range(pieces)
        ]
        for s in range(1, n_dp)
    ]
    hidden_grad = product(down_weight[0], grad_full)
    gate_grad = (hidden_grad * up * sig * (1.0 + gate * (1.0 - sig))).astype(BF16)
    up_grad = (hidden_grad * gate * sig).astype(BF16)

    def columns(target):
        return lax.dynamic_slice(grad_full, (0, target * block), (tokens, block))

    cols = [columns(x)]
    cols.append(mirrored(cols[0]))
    for s in range(1, n_dp):
        got = shifted(columns((x + s) % n_dp), "dp", s)
        cols += [got, mirrored(got)]
    cols = jnp.concatenate(cols, axis=0)
    scale = 32.0 / (2.0 * n_dp * tokens)
    out = []
    for i in range(pieces):
        parts = [hid[i], hid_y[i]]
        for s in range(1, n_dp):
            parts += [hid_x[s - 1][i], hid_d[s - 1][i]]
        total = jnp.dot(jnp.concatenate(parts, axis=1), cols, preferred_element_type=F32)
        out.append((total * scale).astype(BF16))
    weight_grad = jnp.concatenate(out, axis=0)
    return gate_grad[None, None], up_grad[None, None], weight_grad[None]


def solution(mesh):
    in_specs = (
        P("pipe", "dp", None, "tensor"),
        P("pipe", "dp", "tensor", None),
        P("pipe", "dp", "tensor", None),
        P("pipe", "tensor", None),
    )
    out_specs = (
        P("pipe", "dp", "tensor", None),
        P("pipe", "dp", "tensor", None),
        P("pipe", "tensor", "dp"),
    )
    return jax.shard_map(
        on_device, mesh=mesh, in_specs=in_specs, out_specs=out_specs, check_vma=False
    )
```

profile of v0, /device:TPU:0, one launch (start us, length us, event | category | flops | bytes accessed | tf_op | source)
XLA Modules:
  0.0 64.3 jit_solution(17924029669455602309)
XLA Ops:
  0.6 4.1 %collective-permute-start = (bf16[128,640]{1,0:T(8,128)(2,1)}, bf16[128,640]{1,0:T(8,128)(2,1)S(1)}, u32[]{:S(2)}, u32[]{:S(2)}) collective-permute-start(bf16[128,640]{1,0:T(8,128)(2,1)} %bitcast.3), channel_id=1, source_target_pairs={{0,4},{2,6},{4,0},{6,2},{1,5},{3,7},{5,1},{7,3},{8,12},{10,14},{12... | collective-permute-start | bytes 491528 | tf_op jit(solution)/shard_map/ppermute | solution.py:21
  4.8 2.8 %hidden.1 = (bf16[1728,128]{1,0:T(8,128)(2,1)}, bf16[1728,128]{1,0:T(8,128)(2,1)}, bf16[864,128]{1,0:T(8,128)(2,1)}, bf16[864,128]{1,0:T(8,128)(2,1)}, bf16[864,...) custom-call(bf16[1,1,3456,128]{3,2,1,0:T(8,128)(2,1)} %gate_hbm.1, bf16[1,1,3456,128]{3,2,1,0:T(8,128)(2,1)} %up_hbm.1), custom_call_target="tpu_custom_call" | custom-call | flops 7077888 | bytes 2654208 | tf_op jit(solution)/shard_map/hidden/pallas_call | solution.py:67
  7.6 1.6 %collective-permute-start.2 = (bf16[1728,128]{1,0:T(8,128)(2,1)}, bf16[1728,128]{1,0:T(8,128)(2,1)S(1)}, u32[]{:S(2)}, u32[]{:S(2)}) collective-permute-start(bf16[1728,128]{1,0:T(8,128)(2,1)} %get-tuple-element.27.refs_0_), channel_id=1, source_target_pairs={{0,16},{8,24},{16,0},{24,8},{1,17},{9,25},{17,1},{25,9},{2,18},{10... | collective-permute-start | bytes 1327112 | tf_op jit(solution)/shard_map/ppermute | solution.py:21
  9.2 1.5 %collective-permute-start.4 = (bf16[1728,128]{1,0:T(8,128)(2,1)}, bf16[1728,128]{1,0:T(8,128)(2,1)S(1)}, u32[]{:S(2)}, u32[]{:S(2)}) collective-permute-start(bf16[1728,128]{1,0:T(8,128)(2,1)} %get-tuple-element.29.refs_4_), channel_id=1, source_target_pairs={{0,1},{1,0},{2,3},{3,2},{4,5},{5,4},{6,7},{7,6},{8,9},{9,8},{10,11... | collective-permute-start | bytes 1327112 | tf_op jit(solution)/shard_map/ppermute | solution.py:17
  10.7 0.0 copy-start.4
  10.7 0.9 %copy-done.4 = bf16[1,1,128,640]{3,2,1,0:T(8,128)(2,1)S(1)} copy-done((bf16[1,1,128,640]{3,2,1,0:T(8,128)(2,1)S(1)}, bf16[1,1,128,640]{3,2,1,0:T(8,128)(2,1)}, u32[]{:S(2)}) %copy-start.4) | copy-done | bytes 163864
  11.6 0.0 copy-start.8
  11.6 0.0 copy-start.7
  11.6 6.9 %load_all.1 = (bf16[3456,2560]{1,0:T(8,128)(2,1)S(1)}, bf16[128,640]{1,0:T(8,128)(2,1)S(1)}, f32[3456,128]{1,0:T(8,128)S(1)}) custom-call(bf16[1,3456,2560]{2,1,0:T(8,128)(2,1)} %weight_hbm.1, bf16[1,1,128,640]{3,2,1,0:T(8,128)(2,1)S(1)} %copy-done.4), custom_call_target="tpu_custom_call" | custom-call | flops 566231040 | bytes 17694720 | tf_op jit(solution)/shard_map/load_all/pallas_call | solution.py:133
  18.5 0.0 collective-permute-done.far_ref
  18.5 0.1 shard_map.67
  18.6 0.6 collective-permute-start.8
  19.2 0.5 collective-permute-start.9
  19.7 2.5 %collective-permute-start.10 = (bf16[128,640]{1,0:T(8,128)(2,1)S(1)}, bf16[128,640]{1,0:T(8,128)(2,1)S(1)}, u32[]{:S(2)}, u32[]{:S(2)}) collective-permute-start(bf16[128,640]{1,0:T(8,128)(2,1)S(1)} %get-tuple-element.34), channel_id=1, source_target_pairs={{0,17},{1,16},{8,25},{9,24},{16,1},{17,0},{24,9},{25,8},{2,19},{3,... | collective-permute-start | bytes 491528 | tf_op jit(solution)/shard_map/ppermute | solution.py:31
  22.2 3.1 %collective-permute-done.8.refs_0_.refs_9_ = bf16[128,640]{1,0:T(8,128)(2,1)S(1)} collective-permute-done((bf16[128,640]{1,0:T(8,128)(2,1)S(1)}, bf16[128,640]{1,0:T(8,128)(2,1)S(1)}, u32[]{:S(2)}, u32[]{:S(2)}) %collective-permute-start.8) | collective-permute-done | bytes 163872 | tf_op jit(solution)/shard_map/ppermute | solution.py:21
  25.3 0.0 copy-done.8
  25.3 0.1 collective-permute-start.12
  25.4 0.8 %collective-permute-done.9.refs_1_.refs_10_ = bf16[128,640]{1,0:T(8,128)(2,1)S(1)} collective-permute-done((bf16[128,640]{1,0:T(8,128)(2,1)S(1)}, bf16[128,640]{1,0:T(8,128)(2,1)S(1)}, u32[]{:S(2)}, u32[]{:S(2)}) %collective-permute-start.9) | collective-permute-done | bytes 163872 | tf_op jit(solution)/shard_map/ppermute | solution.py:17
  26.2 4.5 %collective-permute-done.10.refs_2_.refs_11_ = bf16[128,640]{1,0:T(8,128)(2,1)S(1)} collective-permute-done((bf16[128,640]{1,0:T(8,128)(2,1)S(1)}, bf16[128,640]{1,0:T(8,128)(2,1)S(1)}, u32[]{:S(2)}, u32[]{:S(2)}) %collective-permute-start.10) | collective-permute-done | bytes 163872 | tf_op jit(solution)/shard_map/ppermute | solution.py:31
  30.8 1.6 %collective-permute-start.11 = (bf16[3,128,640]{2,1,0:T(8,128)(2,1)S(1)}, bf16[3,128,640]{2,1,0:T(8,128)(2,1)S(1)}, u32[]{:S(2)}, u32[]{:S(2)}) collective-permute-start(bf16[3,128,640]{2,1,0:T(8,128)(2,1)S(1)} %shard_map.69), channel_id=1, source_target_pairs={{0,2},{2,0},{4,6},{6,4},{1,3},{3,1},{5,7},{7,5},{8,10},{10,8},{12,... | collective-permute-start | bytes 1474568 | tf_op jit(solution)/shard_map/ppermute | solution.py:21
  32.4 0.4 collective-permute-start.1
  32.9 0.0 collective-permute-done.2.refs_0_.refs_1_
  32.9 0.0 copy-done.7
  32.9 0.5 collective-permute-start.14
  33.4 0.0 collective-permute-done.4.refs_1_.refs_6_
  33.4 0.1 shard_map.68
  33.4 0.8 %collective-permute-start.13 = (bf16[864,128]{1,0:T(8,128)(2,1)S(1)}, bf16[864,128]{1,0:T(8,128)(2,1)S(1)}, u32[]{:S(2)}, u32[]{:S(2)}) collective-permute-start(bf16[864,128]{1,0:T(8,128)(2,1)S(1)} %get-tuple-element.36), channel_id=1, source_target_pairs={{0,1},{1,0},{2,3},{3,2},{4,5},{5,4},{6,7},{7,6},{8,9},{9,8},{10,11... | collective-permute-start | bytes 663560 | tf_op jit(solution)/shard_map/ppermute | solution.py:17
  34.2 0.0 collective-permute-done.12.refs_2_
  34.2 1.4 %collective-permute-start.15 = (bf16[864,128]{1,0:T(8,128)(2,1)S(1)}, bf16[864,128]{1,0:T(8,128)(2,1)S(1)}, u32[]{:S(2)}, u32[]{:S(2)}) collective-permute-start(bf16[864,128]{1,0:T(8,128)(2,1)S(1)} %get-tuple-element.38), channel_id=1, source_target_pairs={{0,16},{8,24},{16,0},{24,8},{1,17},{9,25},{17,1},{25,9},{2,18},{10... | collective-permute-start | bytes 663560 | tf_op jit(solution)/shard_map/ppermute | solution.py:21
  35.6 0.0 copy-start.6
  35.6 0.0 copy-start.5
  35.6 0.0 copy-start
  35.6 0.0 copy-start.1
  35.6 2.0 %input_grads.2.refs_2_ = f32[3456,128]{1,0:T(8,128)S(1)} custom-call(bf16[1,128,640]{2,1,0:T(8,128)(2,1)S(1)} %bitcast.2, bf16[3456,2560]{1,0:T(8,128)(2,1)S(1)} %get-tuple-element.23.refs_1_, f32[3456,128]{1,0:T(8,128)S(1)} %get-tuple-element.24.refs_2_), custom_call_target="tpu_custom_call" | custom-call | flops 566231040 | bytes 4423680 | tf_op jit(solution)/shard_map/input_grads/pallas_call | solution.py:191
  37.5 1.3 %collective-permute-done.14.refs_5_ = bf16[864,128]{1,0:T(8,128)(2,1)S(1)} collective-permute-done((bf16[864,128]{1,0:T(8,128)(2,1)S(1)}, bf16[864,128]{1,0:T(8,128)(2,1)S(1)}, u32[]{:S(2)}, u32[]{:S(2)}) %collective-permute-start.14) | collective-permute-done | bytes 221216 | tf_op jit(solution)/shard_map/ppermute | solution.py:21
  38.8 0.0 copy-done.6
  38.8 1.4 %collective-permute-start.3 = (bf16[864,128]{1,0:T(8,128)(2,1)S(1)}, bf16[864,128]{1,0:T(8,128)(2,1)S(1)}, u32[]{:S(2)}, u32[]{:S(2)}) collective-permute-start(bf16[864,128]{1,0:T(8,128)(2,1)S(1)} %copy-done.6), channel_id=1, source_target_pairs={{0,1},{1,0},{2,3},{3,2},{4,5},{5,4},{6,7},{7,6},{8,9},{9,8},{10,11... | collective-permute-start | bytes 663560 | tf_op jit(solution)/shard_map/ppermute | solution.py:17
  40.2 6.1 %collective-permute-done.1.refs_0_.refs_12_ = bf16[2,128,640]{2,1,0:T(8,128)(2,1)S(1)} collective-permute-done((bf16[2,128,640]{2,1,0:T(8,128)(2,1)S(1)}, bf16[2,128,640]{2,1,0:T(8,128)(2,1)S(1)}, u32[]{:S(2)}, u32[]{:S(2)}) %collective-permute-start.1) | collective-permute-done | bytes 327712 | tf_op jit(solution)/shard_map/ppermute | solution.py:21
  46.3 0.0 copy-done.5
  46.3 1.0 %collective-permute-start.6 = (bf16[864,128]{1,0:T(8,128)(2,1)S(1)}, bf16[864,128]{1,0:T(8,128)(2,1)S(1)}, u32[]{:S(2)}, u32[]{:S(2)}) collective-permute-start(bf16[864,128]{1,0:T(8,128)(2,1)S(1)} %copy-done.5), channel_id=1, source_target_pairs={{0,16},{8,24},{16,0},{24,8},{1,17},{9,25},{17,1},{25,9},{2,18},{10... | collective-permute-start | bytes 663560 | tf_op jit(solution)/shard_map/ppermute | solution.py:21
  47.3 0.0 collective-permute-done.13.refs_3_
  47.3 2.6 %collective-permute-start.5 = (bf16[864,128]{1,0:T(8,128)(2,1)S(1)}, bf16[864,128]{1,0:T(8,128)(2,1)S(1)}, u32[]{:S(2)}, u32[]{:S(2)}) collective-permute-start(bf16[864,128]{1,0:T(8,128)(2,1)S(1)} %get-tuple-element.30), channel_id=1, source_target_pairs={{0,1},{1,0},{2,3},{3,2},{4,5},{5,4},{6,7},{7,6},{8,9},{9,8},{10,11... | collective-permute-start | bytes 663560 | tf_op jit(solution)/shard_map/ppermute | solution.py:17
  49.9 0.0 collective-permute-done.15.refs_7_
  49.9 0.0 copy-start.2
  49.9 0.0 copy-start.3
  49.9 0.1 collective-permute-start.7
  50.0 0.0 copy-done
  50.0 0.0 copy-done.1
  50.0 5.3 %input_grads.3 = (bf16[1,1,3456,128]{3,2,1,0:T(8,128)(2,1)}, bf16[1,1,3456,128]{3,2,1,0:T(8,128)(2,1)}) custom-call(bf16[2,128,640]{2,1,0:T(8,128)(2,1)S(1)} %collective-permute-done.1.refs_0_.refs_12_, bf16[3456,2560]{1,0:T(8,128)(2,1)S(1)} %get-tuple-element.23.refs_1_, f32[3456,128]{1,0:T(8,128)S(1)} %input_grads.2.refs_2_, ...), custom_call_target="tpu_custom_call" | custom-call | flops 1132462080 | bytes 8847360 | tf_op jit(solution)/shard_map/input_grads/pallas_call | solution.py:191
  55.2 0.0 collective-permute-done.11.refs_13_
  55.2 0.0 copy-done.2
  55.2 0.0 copy-done.3
  55.3 4.5 %weight_rows.2.refs_14_ = bf16[1,3456,1280]{2,1,0:T(8,128)(2,1)} custom-call(bf16[1728,128]{1,0:T(8,128)(2,1)S(1)} %copy-done.2, bf16[1728,128]{1,0:T(8,128)(2,1)S(1)} %collective-permute-done.2.refs_0_.refs_1_, bf16[864,128]{1,0:T(8,128)(2,1)S(1)} %collective-permute-done.12.refs_2_, bf16[864,128]{1,0:T(8,128)(2,1)S(1)} %collective-permute-done.13.refs_3_, ...), custom_call_target="tpu_custom_call" | custom-call | flops 2264924160 | bytes 6193152 | tf_op jit(solution)/shard_map/weight_rows/pallas_call | solution.py:299
  59.8 0.0 collective-permute-done.3.refs_2_
  59.8 0.0 collective-permute-done.6.refs_5_
  59.8 0.0 collective-permute-done.5.refs_3_
  59.8 0.0 collective-permute-done.7.refs_7_
  59.8 4.5 %weight_rows.3 = bf16[1,3456,1280]{2,1,0:T(8,128)(2,1)} custom-call(bf16[1728,128]{1,0:T(8,128)(2,1)S(1)} %copy-done.2, bf16[1728,128]{1,0:T(8,128)(2,1)S(1)} %collective-permute-done.2.refs_0_.refs_1_, bf16[864,128]{1,0:T(8,128)(2,1)S(1)} %collective-permute-done.3.refs_2_, ...), custom_call_target="tpu_custom_call", output_to_operand_aliasing={{}: (14, {})} | custom-call | flops 2264924160 | bytes 6193152 | tf_op jit(solution)/shard_map/weight_rows/pallas_call | solution.py:299
  (1 shorter events, 0.0 us)
Async XLA Ops:
  0.6 17.9 %collective-permute-start = (bf16[128,640]{1,0:T(8,128)(2,1)}, bf16[128,640]{1,0:T(8,128)(2,1)S(1)}, u32[]{:S(2)}, u32[]{:S(2)}) collective-permute-start(bf16[128,640]{1,0:T(8,128)(2,1)} %bitcast.3), channel_id=1, source_target_pairs={{0,4},{2,6},{4,0},{6,2},{1,5},{3,7},{5,1},{7,3},{8,12},{10,14},{12... | collective-permute-start | bytes 491528 | tf_op jit(solution)/shard_map/ppermute | solution.py:21
  7.6 25.3 %collective-permute-start.2 = (bf16[1728,128]{1,0:T(8,128)(2,1)}, bf16[1728,128]{1,0:T(8,128)(2,1)S(1)}, u32[]{:S(2)}, u32[]{:S(2)}) collective-permute-start(bf16[1728,128]{1,0:T(8,128)(2,1)} %get-tuple-element.27.refs_0_), channel_id=1, source_target_pairs={{0,16},{8,24},{16,0},{24,8},{1,17},{9,25},{17,1},{25,9},{2,18},{10... | collective-permute-start | bytes 1327112 | tf_op jit(solution)/shard_map/ppermute | solution.py:21
  9.2 24.2 %collective-permute-start.4 = (bf16[1728,128]{1,0:T(8,128)(2,1)}, bf16[1728,128]{1,0:T(8,128)(2,1)S(1)}, u32[]{:S(2)}, u32[]{:S(2)}) collective-permute-start(bf16[1728,128]{1,0:T(8,128)(2,1)} %get-tuple-element.29.refs_4_), channel_id=1, source_target_pairs={{0,1},{1,0},{2,3},{3,2},{4,5},{5,4},{6,7},{7,6},{8,9},{9,8},{10,11... | collective-permute-start | bytes 1327112 | tf_op jit(solution)/shard_map/ppermute | solution.py:17
  10.7 0.9 %copy-start.4 = (bf16[1,1,128,640]{3,2,1,0:T(8,128)(2,1)S(1)}, bf16[1,1,128,640]{3,2,1,0:T(8,128)(2,1)}, u32[]{:S(2)}) copy-start(bf16[1,1,128,640]{3,2,1,0:T(8,128)(2,1)} %own_hbm.1) | copy-start | bytes 491524
  11.6 13.7 %copy-start.8 = (bf16[864,128]{1,0:T(8,128)(2,1)S(1)}, bf16[864,128]{1,0:T(8,128)(2,1)}, u32[]{:S(2)}) copy-start(bf16[864,128]{1,0:T(8,128)(2,1)} %get-tuple-element.35) | copy-start | bytes 663556
  11.6 21.3 %copy-start.7 = (bf16[864,128]{1,0:T(8,128)(2,1)S(1)}, bf16[864,128]{1,0:T(8,128)(2,1)}, u32[]{:S(2)}) copy-start(bf16[864,128]{1,0:T(8,128)(2,1)} %get-tuple-element.37) | copy-start | bytes 663556
  18.6 6.7 %collective-permute-start.8 = (bf16[128,640]{1,0:T(8,128)(2,1)S(1)}, bf16[128,640]{1,0:T(8,128)(2,1)S(1)}, u32[]{:S(2)}, u32[]{:S(2)}) collective-permute-start(bf16[128,640]{1,0:T(8,128)(2,1)S(1)} %get-tuple-element.33.refs_8_), channel_id=1, source_target_pairs={{0,16},{8,24},{16,0},{24,8},{1,17},{9,25},{17,1},{25,9},{2,18},{10... | collective-permute-start | bytes 491528 | tf_op jit(solution)/shard_map/ppermute | solution.py:21
  19.2 7.1 %collective-permute-start.9 = (bf16[128,640]{1,0:T(8,128)(2,1)S(1)}, bf16[128,640]{1,0:T(8,128)(2,1)S(1)}, u32[]{:S(2)}, u32[]{:S(2)}) collective-permute-start(bf16[128,640]{1,0:T(8,128)(2,1)S(1)} %get-tuple-element.34), channel_id=1, source_target_pairs={{0,1},{1,0},{2,3},{3,2},{4,5},{5,4},{6,7},{7,6},{8,9},{9,8},{10,11... | collective-permute-start | bytes 491528 | tf_op jit(solution)/shard_map/ppermute | solution.py:17
  19.7 11.0 %collective-permute-start.10 = (bf16[128,640]{1,0:T(8,128)(2,1)S(1)}, bf16[128,640]{1,0:T(8,128)(2,1)S(1)}, u32[]{:S(2)}, u32[]{:S(2)}) collective-permute-start(bf16[128,640]{1,0:T(8,128)(2,1)S(1)} %get-tuple-element.34), channel_id=1, source_target_pairs={{0,17},{1,16},{8,25},{9,24},{16,1},{17,0},{24,9},{25,8},{2,19},{3,... | collective-permute-start | bytes 491528 | tf_op jit(solution)/shard_map/ppermute | solution.py:31
  25.3 8.9 %collective-permute-start.12 = (bf16[864,128]{1,0:T(8,128)(2,1)S(1)}, bf16[864,128]{1,0:T(8,128)(2,1)S(1)}, u32[]{:S(2)}, u32[]{:S(2)}) collective-permute-start(bf16[864,128]{1,0:T(8,128)(2,1)S(1)} %copy-done.8), channel_id=1, source_target_pairs={{0,1},{1,0},{2,3},{3,2},{4,5},{5,4},{6,7},{7,6},{8,9},{9,8},{10,11... | collective-permute-start | bytes 663560 | tf_op jit(solution)/shard_map/ppermute | solution.py:17
  30.8 24.5 %collective-permute-start.11 = (bf16[3,128,640]{2,1,0:T(8,128)(2,1)S(1)}, bf16[3,128,640]{2,1,0:T(8,128)(2,1)S(1)}, u32[]{:S(2)}, u32[]{:S(2)}) collective-permute-start(bf16[3,128,640]{2,1,0:T(8,128)(2,1)S(1)} %shard_map.69), channel_id=1, source_target_pairs={{0,2},{2,0},{4,6},{6,4},{1,3},{3,1},{5,7},{7,5},{8,10},{10,8},{12,... | collective-permute-start | bytes 1474568 | tf_op jit(solution)/shard_map/ppermute | solution.py:21
  32.4 13.9 %collective-permute-start.1 = (bf16[2,128,640]{2,1,0:T(8,128)(2,1)S(1)}, bf16[2,128,640]{2,1,0:T(8,128)(2,1)S(1)}, u32[]{:S(2)}, u32[]{:S(2)}) collective-permute-start(bf16[2,128,640]{2,1,0:T(8,128)(2,1)S(1)} %get-tuple-element.22), channel_id=1, source_target_pairs={{0,2},{2,0},{4,6},{6,4},{1,3},{3,1},{5,7},{7,5},{8,10},{10,8},{12,... | collective-permute-start | bytes 983048 | tf_op jit(solution)/shard_map/ppermute | solution.py:21
  32.9 5.9 %collective-permute-start.14 = (bf16[864,128]{1,0:T(8,128)(2,1)S(1)}, bf16[864,128]{1,0:T(8,128)(2,1)S(1)}, u32[]{:S(2)}, u32[]{:S(2)}) collective-permute-start(bf16[864,128]{1,0:T(8,128)(2,1)S(1)} %copy-done.7), channel_id=1, source_target_pairs={{0,16},{8,24},{16,0},{24,8},{1,17},{9,25},{17,1},{25,9},{2,18},{10... | collective-permute-start | bytes 663560 | tf_op jit(solution)/shard_map/ppermute | solution.py:21
  33.4 13.9 %collective-permute-start.13 = (bf16[864,128]{1,0:T(8,128)(2,1)S(1)}, bf16[864,128]{1,0:T(8,128)(2,1)S(1)}, u32[]{:S(2)}, u32[]{:S(2)}) collective-permute-start(bf16[864,128]{1,0:T(8,128)(2,1)S(1)} %get-tuple-element.36), channel_id=1, source_target_pairs={{0,1},{1,0},{2,3},{3,2},{4,5},{5,4},{6,7},{7,6},{8,9},{9,8},{10,11... | collective-permute-start | bytes 663560 | tf_op jit(solution)/shard_map/ppermute | solution.py:17
  34.2 15.7 %collective-permute-start.15 = (bf16[864,128]{1,0:T(8,128)(2,1)S(1)}, bf16[864,128]{1,0:T(8,128)(2,1)S(1)}, u32[]{:S(2)}, u32[]{:S(2)}) collective-permute-start(bf16[864,128]{1,0:T(8,128)(2,1)S(1)} %get-tuple-element.38), channel_id=1, source_target_pairs={{0,16},{8,24},{16,0},{24,8},{1,17},{9,25},{17,1},{25,9},{2,18},{10... | collective-permute-start | bytes 663560 | tf_op jit(solution)/shard_map/ppermute | solution.py:21
  35.6 3.2 %copy-start.6 = (bf16[864,128]{1,0:T(8,128)(2,1)S(1)}, bf16[864,128]{1,0:T(8,128)(2,1)}, u32[]{:S(2)}) copy-start(bf16[864,128]{1,0:T(8,128)(2,1)} %get-tuple-element.28) | copy-start | bytes 663556
  35.6 10.7 %copy-start.5 = (bf16[864,128]{1,0:T(8,128)(2,1)S(1)}, bf16[864,128]{1,0:T(8,128)(2,1)}, u32[]{:S(2)}) copy-start(bf16[864,128]{1,0:T(8,128)(2,1)} %get-tuple-element.31) | copy-start | bytes 663556
  35.6 14.4 %copy-start = (bf16[1,1,3456,128]{3,2,1,0:T(8,128)(2,1)S(1)}, bf16[1,1,3456,128]{3,2,1,0:T(8,128)(2,1)}, u32[]{:S(2)}) copy-start(bf16[1,1,3456,128]{3,2,1,0:T(8,128)(2,1)} %gate_hbm.1) | copy-start | bytes 2654212
  35.6 14.4 %copy-start.1 = (bf16[1,1,3456,128]{3,2,1,0:T(8,128)(2,1)S(1)}, bf16[1,1,3456,128]{3,2,1,0:T(8,128)(2,1)}, u32[]{:S(2)}) copy-start(bf16[1,1,3456,128]{3,2,1,0:T(8,128)(2,1)} %up_hbm.1) | copy-start | bytes 2654212
  38.8 21.0 %collective-permute-start.3 = (bf16[864,128]{1,0:T(8,128)(2,1)S(1)}, bf16[864,128]{1,0:T(8,128)(2,1)S(1)}, u32[]{:S(2)}, u32[]{:S(2)}) collective-permute-start(bf16[864,128]{1,0:T(8,128)(2,1)S(1)} %copy-done.6), channel_id=1, source_target_pairs={{0,1},{1,0},{2,3},{3,2},{4,5},{5,4},{6,7},{7,6},{8,9},{9,8},{10,11... | collective-permute-start | bytes 663560 | tf_op jit(solution)/shard_map/ppermute | solution.py:17
  46.3 13.5 %collective-permute-start.6 = (bf16[864,128]{1,0:T(8,128)(2,1)S(1)}, bf16[864,128]{1,0:T(8,128)(2,1)S(1)}, u32[]{:S(2)}, u32[]{:S(2)}) collective-permute-start(bf16[864,128]{1,0:T(8,128)(2,1)S(1)} %copy-done.5), channel_id=1, source_target_pairs={{0,16},{8,24},{16,0},{24,8},{1,17},{9,25},{17,1},{25,9},{2,18},{10... | collective-permute-start | bytes 663560 | tf_op jit(solution)/shard_map/ppermute | solution.py:21
  47.3 12.5 %collective-permute-start.5 = (bf16[864,128]{1,0:T(8,128)(2,1)S(1)}, bf16[864,128]{1,0:T(8,128)(2,1)S(1)}, u32[]{:S(2)}, u32[]{:S(2)}) collective-permute-start(bf16[864,128]{1,0:T(8,128)(2,1)S(1)} %get-tuple-element.30), channel_id=1, source_target_pairs={{0,1},{1,0},{2,3},{3,2},{4,5},{5,4},{6,7},{7,6},{8,9},{9,8},{10,11... | collective-permute-start | bytes 663560 | tf_op jit(solution)/shard_map/ppermute | solution.py:17
  49.9 5.4 %copy-start.2 = (bf16[1728,128]{1,0:T(8,128)(2,1)S(1)}, bf16[1728,128]{1,0:T(8,128)(2,1)}, u32[]{:S(2)}) copy-start(bf16[1728,128]{1,0:T(8,128)(2,1)} %get-tuple-element.27.refs_0_) | copy-start | bytes 1327108
  49.9 5.4 %copy-start.3 = (bf16[1728,128]{1,0:T(8,128)(2,1)S(1)}, bf16[1728,128]{1,0:T(8,128)(2,1)}, u32[]{:S(2)}) copy-start(bf16[1728,128]{1,0:T(8,128)(2,1)} %get-tuple-element.29.refs_4_) | copy-start | bytes 1327108
  49.9 9.9 %collective-permute-start.7 = (bf16[864,128]{1,0:T(8,128)(2,1)S(1)}, bf16[864,128]{1,0:T(8,128)(2,1)S(1)}, u32[]{:S(2)}, u32[]{:S(2)}) collective-permute-start(bf16[864,128]{1,0:T(8,128)(2,1)S(1)} %get-tuple-element.32), channel_id=1, source_target_pairs={{0,16},{8,24},{16,0},{24,8},{1,17},{9,25},{17,1},{25,9},{2,18},{10... | collective-permute-start | bytes 663560 | tf_op jit(solution)/shard_map/ppermute | solution.py:21
where the time goes:
time: 64.5 us; the launch traced here: 64.3 us
  Pallas kernels  26.2 us (41%)
  starting transfers between devices  20.7 us (32%)
  waiting for transfers between devices  15.8 us (24%)
  local copies, waits for them, and re-layouts  0.94 us (1%)
  between operations  0.73 us (1%)
    ppermute x9, starting transfers between devices, crossed(): lax.ppermute(value, axis, [(i, i ^ mask) for i in range(lax.axis_size(axi...  11.3 us
    ppermute x9, waiting for transfers between devices, crossed(): lax.ppermute(value, axis, [(i, i ^ mask) for i in range(lax.axis_size(axi...  10.5 us
    pallas_call x2, Pallas kernels, weight_rows(): pl.pallas_call(functools.partial(weight_kernel, scale, [first for _, firs...  9.02 us
    pallas_call x2, Pallas kernels, input_grads(): pl.pallas_call(functools.partial(grads_kernel, flips, tile), grid=(rows /...  7.23 us
    pallas_call x1, Pallas kernels, load_all(): pl.pallas_call(functools.partial(load_kernel, tile), in_specs=[hbm] * 2,...  6.93 us
    ppermute x6, starting transfers between devices, shifted(): lax.ppermute(value, axis, [(i, (i + step) % size) for i in range(size)])  6.93 us
    ppermute x1, waiting for transfers between devices, opposite(): lax.ppermute(value, ('pipe', 'dp'), [(i, i ^ mask) for i in range(n_pipe...  4.47 us
    pallas_call x1, Pallas kernels, hidden_pieces(): pl.pallas_call(functools.partial(hidden_kernel, cuts), in_specs=[pl.Block...  2.82 us
  transfers between devices with their start and end apart: 16, of which 5 were waited for; matrix products, arithmetic and copies ran while one was open for 0% of the time, Pallas kernels for 34%

commit v1 on v0

--- a/solution.py
+++ b/solution.py
@@ -33,7 +33,8 @@
     )
 
 
-HIDDEN_LIMIT = 60 << 20
+HIDDEN_LIMIT = 52 << 20
+TILE = 576
 LOAD_LIMIT = 30 << 20
 GRADS_LIMIT = 6 << 20
 
@@ -319,7 +320,7 @@
     tokens, _ = own.shape
     rows = gate_pre.shape[2]
     half = rows // 2
-    pieces = (0, half // 2, half)
+    pieces = (0, half * 2 // 3, half)
 
     def to_x(value):
         return shifted(value, "dp", 1)
@@ -351,7 +352,7 @@
     b_d = [mirrored(cuts[n + k]) for k in range(n)]
     a_x = [to_x(hid[k]) for k in range(n)]
     b_y = [mirrored(hid[n + k]) for k in range(n)]
-    gate_grad, up_grad = input_grads(pair_other, (1, 3), rows // 8, weight, acc, gate_pre, up_pre)
+    gate_grad, up_grad = input_grads(pair_other, (1, 3), rows // 4, weight, acc, gate_pre, up_pre)
     scale = 32.0 / (2.0 * 2 * tokens)
     out = None
     for k in range(n):
@@ -365,7 +366,7 @@
             pieces[k + 1] - first,
             [mine, g_y, g_x, g_d, pair_other, g_other],
             scale,
-            half // 4,
+            TILE,
             out,
         )
     return gate_grad, up_grad, out

time: 64.5 us -> 72.2 us (1.12)
  local copies, waits for them, and re-layouts: 0.94 us -> 13.1 us
  Pallas kernels: 26.2 us -> 23 us
  waiting for transfers between devices: 15.8 us -> 13 us
  starting transfers between devices: 20.7 us -> 22.2 us
    unnamed x18 -> x10, local copies, waits for them, and re-layouts: 0.94 us -> 13.1 us
    ppermute x9, waiting for transfers between devices: 10.5 us -> 0.02 us  [crossed(): lax.ppermute(value, axis, [(i, i ^ mask) for i in range(lax.axis_size(axi...]
    ppermute x6, waiting for transfers between devices: 0.84 us -> 10.3 us  [shifted(): lax.ppermute(value, axis, [(i, (i + step) % size) for i in range(size)])]
    ppermute x9, starting transfers between devices: 11.3 us -> 13.6 us  [crossed(): lax.ppermute(value, axis, [(i, i ^ mask) for i in range(lax.axis_size(axi...]
    ppermute x1, waiting for transfers between devices: 4.47 us -> 2.71 us  [opposite(): lax.ppermute(value, ('pipe', 'dp'), [(i, i ^ mask) for i in range(n_pipe...]
    pallas_call x2, Pallas kernels: 7.23 us -> 5.94 us  [input_grads(): pl.pallas_call(functools.partial(grads_kernel, flips, tile), grid=(rows /...]
    pallas_call x1, Pallas kernels: 2.82 us -> 1.62 us  [hidden_pieces(): pl.pallas_call(functools.partial(hidden_kernel, cuts), in_specs=[pl.Block...]
    ppermute x6, starting transfers between devices: 6.93 us -> 6.14 us  [shifted(): lax.ppermute(value, axis, [(i, (i + step) % size) for i in range(size)])]
  transfers between devices with their start and end apart: 16 -> 16, of which waited for: 5 -> 2; matrix products, arithmetic and copies ran while one was open for 0% -> 0% of each run, Pallas kernels for 34% -> 27%
where the time goes in v1:
time: 72.2 us; the launch traced here: 72 us
  Pallas kernels  23 us (32%)
  starting transfers between devices  22.2 us (31%)
  local copies, waits for them, and re-layouts  13.1 us (18%)
  waiting for transfers between devices  13 us (18%)
    ppermute x9, starting transfers between devices, crossed(): lax.ppermute(value, axis, [(i, i ^ mask) for i in range(lax.axis_size(axi...  13.6 us
    unnamed x10, local copies, waits for them, and re-layouts  13.1 us
    ppermute x6, waiting for transfers between devices, shifted(): lax.ppermute(value, axis, [(i, (i + step) % size) for i in range(size)])  10.3 us
    pallas_call x2, Pallas kernels, weight_rows(): pl.pallas_call(functools.partial(weight_kernel, scale, [first for _, firs...  8.45 us
    pallas_call x1, Pallas kernels, load_all(): pl.pallas_call(functools.partial(load_kernel, tile), in_specs=[hbm] * 2,...  6.89 us
    ppermute x6, starting transfers between devices, shifted(): lax.ppermute(value, axis, [(i, (i + step) % size) for i in range(size)])  6.14 us
    pallas_call x2, Pallas kernels, input_grads(): pl.pallas_call(functools.partial(grads_kernel, flips, tile), grid=(rows /...  5.94 us
    ppermute x1, waiting for transfers between devices, opposite(): lax.ppermute(value, ('pipe', 'dp'), [(i, i ^ mask) for i in range(n_pipe...  2.71 us
  transfers between devices with their start and end apart: 16, of which 2 were waited for; matrix products, arithmetic and copies ran while one was open for 0% of the time, Pallas kernels for 27%

profile of v1, /device:TPU:0, one launch (start us, length us, event | category | flops | bytes accessed | tf_op | source)
XLA Modules:
  0.0 72.0 jit_solution(15009912864140612249)
XLA Ops:
  0.6 4.1 %collective-permute-start = (bf16[128,640]{1,0:T(8,128)(2,1)}, bf16[128,640]{1,0:T(8,128)(2,1)S(1)}, u32[]{:S(2)}, u32[]{:S(2)}) collective-permute-start(bf16[128,640]{1,0:T(8,128)(2,1)} %bitcast.3), channel_id=1, source_target_pairs={{0,4},{2,6},{4,0},{6,2},{1,5},{3,7},{5,1},{7,3},{8,12},{10,14},{12... | collective-permute-start | bytes 491528 | tf_op jit(solution)/shard_map/ppermute | solution.py:21
  4.8 0.0 copy-start.4
  4.8 0.9 %copy-done.4 = bf16[1,1,128,640]{3,2,1,0:T(8,128)(2,1)S(1)} copy-done((bf16[1,1,128,640]{3,2,1,0:T(8,128)(2,1)S(1)}, bf16[1,1,128,640]{3,2,1,0:T(8,128)(2,1)}, u32[]{:S(2)}) %copy-start.4) | copy-done | bytes 163864
  5.7 6.9 %load_all.1 = (bf16[3456,2560]{1,0:T(8,128)(2,1)S(1)}, bf16[128,640]{1,0:T(8,128)(2,1)S(1)}, f32[3456,128]{1,0:T(8,128)S(1)}) custom-call(bf16[1,3456,2560]{2,1,0:T(8,128)(2,1)} %weight_hbm.1, bf16[1,1,128,640]{3,2,1,0:T(8,128)(2,1)S(1)} %copy-done.4), custom_call_target="tpu_custom_call" | custom-call | flops 566231040 | bytes 17694720 | tf_op jit(solution)/shard_map/load_all/pallas_call | solution.py:134
  12.6 0.0 copy-start
  12.6 6.1 %copy-done = bf16[3456,2560]{1,0:T(8,128)(2,1)} copy-done((bf16[3456,2560]{1,0:T(8,128)(2,1)}, bf16[3456,2560]{1,0:T(8,128)(2,1)S(1)}, u32[]{:S(2)}) %copy-start) | copy-done | bytes 17694744
  18.7 0.0 collective-permute-done.far_ref
  18.7 0.1 shard_map.67
  18.7 1.6 %collective-permute-start.8 = (bf16[128,640]{1,0:T(8,128)(2,1)S(1)}, bf16[128,640]{1,0:T(8,128)(2,1)S(1)}, u32[]{:S(2)}, u32[]{:S(2)}) collective-permute-start(bf16[128,640]{1,0:T(8,128)(2,1)S(1)} %get-tuple-element.33.refs_8_), channel_id=1, source_target_pairs={{0,16},{8,24},{16,0},{24,8},{1,17},{9,25},{17,1},{25,9},{2,18},{10... | collective-permute-start | bytes 491528 | tf_op jit(solution)/shard_map/ppermute | solution.py:21
  20.3 1.6 %hidden.1 = (bf16[1728,128]{1,0:T(8,128)(2,1)S(1)}, bf16[1728,128]{1,0:T(8,128)(2,1)S(1)}, bf16[1152,128]{1,0:T(8,128)(2,1)S(1)}, bf16[576,128]{1,0:T(8,128)(2,1...) custom-call(bf16[1,1,3456,128]{3,2,1,0:T(8,128)(2,1)} %gate_hbm.1, bf16[1,1,3456,128]{3,2,1,0:T(8,128)(2,1)} %up_hbm.1), custom_call_target="tpu_custom_call" | custom-call | flops 7077888 | bytes 2654208 | tf_op jit(solution)/shard_map/hidden/pallas_call | solution.py:68
  22.0 0.6 collective-permute-start.2
  22.5 1.5 %collective-permute-start.4 = (bf16[1728,128]{1,0:T(8,128)(2,1)S(1)}, bf16[1728,128]{1,0:T(8,128)(2,1)S(1)}, u32[]{:S(2)}, u32[]{:S(2)}) collective-permute-start(bf16[1728,128]{1,0:T(8,128)(2,1)S(1)} %get-tuple-element.29.refs_4_), channel_id=1, source_target_pairs={{0,1},{1,0},{2,3},{3,2},{4,5},{5,4},{6,7},{7,6},{8,9},{9,8},{10,11... | collective-permute-start | bytes 1327112 | tf_op jit(solution)/shard_map/ppermute | solution.py:17
  24.0 0.5 collective-permute-start.9
  24.6 2.4 %collective-permute-start.10 = (bf16[128,640]{1,0:T(8,128)(2,1)S(1)}, bf16[128,640]{1,0:T(8,128)(2,1)S(1)}, u32[]{:S(2)}, u32[]{:S(2)}) collective-permute-start(bf16[128,640]{1,0:T(8,128)(2,1)S(1)} %get-tuple-element.34), channel_id=1, source_target_pairs={{0,17},{1,16},{8,25},{9,24},{16,1},{17,0},{24,9},{25,8},{2,19},{3,... | collective-permute-start | bytes 491528 | tf_op jit(solution)/shard_map/ppermute | solution.py:31
  27.0 0.0 collective-permute-done.8.refs_0_.refs_9_
  27.0 1.6 %collective-permute-start.1 = (bf16[2,128,640]{2,1,0:T(8,128)(2,1)S(1)}, bf16[2,128,640]{2,1,0:T(8,128)(2,1)S(1)}, u32[]{:S(2)}, u32[]{:S(2)}) collective-permute-start(bf16[2,128,640]{2,1,0:T(8,128)(2,1)S(1)} %get-tuple-element.22), channel_id=1, source_target_pairs={{0,2},{2,0},{4,6},{6,4},{1,3},{3,1},{5,7},{7,5},{8,10},{10,8},{12,... | collective-permute-start | bytes 983048 | tf_op jit(solution)/shard_map/ppermute | solution.py:21
  28.6 10.3 %collective-permute-done.9.refs_1_.refs_10_ = bf16[128,640]{1,0:T(8,128)(2,1)S(1)} collective-permute-done((bf16[128,640]{1,0:T(8,128)(2,1)S(1)}, bf16[128,640]{1,0:T(8,128)(2,1)S(1)}, u32[]{:S(2)}, u32[]{:S(2)}) %collective-permute-start.9) | collective-permute-done | bytes 163872 | tf_op jit(solution)/shard_map/ppermute | solution.py:17
  38.9 2.7 %collective-permute-done.10.refs_2_.refs_11_ = bf16[128,640]{1,0:T(8,128)(2,1)S(1)} collective-permute-done((bf16[128,640]{1,0:T(8,128)(2,1)S(1)}, bf16[128,640]{1,0:T(8,128)(2,1)S(1)}, u32[]{:S(2)}, u32[]{:S(2)}) %collective-permute-start.10) | collective-permute-done | bytes 163872 | tf_op jit(solution)/shard_map/ppermute | solution.py:31
  41.6 1.6 %collective-permute-start.11 = (bf16[3,128,640]{2,1,0:T(8,128)(2,1)S(1)}, bf16[3,128,640]{2,1,0:T(8,128)(2,1)S(1)}, u32[]{:S(2)}, u32[]{:S(2)}) collective-permute-start(bf16[3,128,640]{2,1,0:T(8,128)(2,1)S(1)} %shard_map.69), channel_id=1, source_target_pairs={{0,2},{2,0},{4,6},{6,4},{1,3},{3,1},{5,7},{7,5},{8,10},{10,8},{12,... | collective-permute-start | bytes 1474568 | tf_op jit(solution)/shard_map/ppermute | solution.py:21
  43.3 1.5 %collective-permute-start.12 = (bf16[1152,128]{1,0:T(8,128)(2,1)S(1)}, bf16[1152,128]{1,0:T(8,128)(2,1)S(1)}, u32[]{:S(2)}, u32[]{:S(2)}) collective-permute-start(bf16[1152,128]{1,0:T(8,128)(2,1)S(1)} %get-tuple-element.35), channel_id=1, source_target_pairs={{0,1},{1,0},{2,3},{3,2},{4,5},{5,4},{6,7},{7,6},{8,9},{9,8},{10,11... | collective-permute-start | bytes 884744 | tf_op jit(solution)/shard_map/ppermute | solution.py:17
  44.7 0.0 collective-permute-done.2.refs_0_.refs_1_
  44.8 0.5 collective-permute-start.14
  45.3 0.0 collective-permute-done.4.refs_1_.refs_6_
  45.3 0.1 shard_map.68
  45.3 0.6 collective-permute-start.13
  45.9 0.0 collective-permute-done.1.refs_0_.refs_12_
  45.9 1.5 %collective-permute-start.15 = (bf16[1152,128]{1,0:T(8,128)(2,1)S(1)}, bf16[1152,128]{1,0:T(8,128)(2,1)S(1)}, u32[]{:S(2)}, u32[]{:S(2)}) collective-permute-start(bf16[1152,128]{1,0:T(8,128)(2,1)S(1)} %get-tuple-element.38), channel_id=1, source_target_pairs={{0,16},{8,24},{16,0},{24,8},{1,17},{9,25},{17,1},{25,9},{2,18},{10... | collective-permute-start | bytes 884744 | tf_op jit(solution)/shard_map/ppermute | solution.py:21
  47.5 0.0 copy-start.1
  47.5 6.0 %copy-done.1 = bf16[3456,2560]{1,0:T(8,128)(2,1)S(1)} copy-done((bf16[3456,2560]{1,0:T(8,128)(2,1)S(1)}, bf16[3456,2560]{1,0:T(8,128)(2,1)}, u32[]{:S(2)}) %copy-start.1) | copy-done | bytes 17694744
  53.5 0.0 copy-start.2
  53.5 0.0 copy-start.3
  53.5 1.9 %input_grads.2.refs_2_ = f32[3456,128]{1,0:T(8,128)S(1)} custom-call(bf16[1,128,640]{2,1,0:T(8,128)(2,1)S(1)} %bitcast.2, bf16[3456,2560]{1,0:T(8,128)(2,1)S(1)} %copy-done.1, f32[3456,128]{1,0:T(8,128)S(1)} %get-tuple-element.24.refs_2_), custom_call_target="tpu_custom_call" | custom-call | flops 566231040 | bytes 4423680 | tf_op jit(solution)/shard_map/input_grads/pallas_call | solution.py:192
  55.4 0.0 copy-done.2
  55.4 0.0 copy-done.3
  55.5 4.0 %input_grads.3 = (bf16[1,1,3456,128]{3,2,1,0:T(8,128)(2,1)}, bf16[1,1,3456,128]{3,2,1,0:T(8,128)(2,1)}) custom-call(bf16[2,128,640]{2,1,0:T(8,128)(2,1)S(1)} %collective-permute-done.1.refs_0_.refs_12_, bf16[3456,2560]{1,0:T(8,128)(2,1)S(1)} %copy-done.1, f32[3456,128]{1,0:T(8,128)S(1)} %input_grads.2.refs_2_, bf16[1,1,3456,128]{3,2,1,0:T(8,128)(2,1)S(1)} %copy-done.2, ...), custom_call_target="tpu_custom_call" | custom-call | flops 1132462080 | bytes 8847360 | tf_op jit(solution)/shard_map/input_grads/pallas_call | solution.py:192
  59.5 0.0 collective-permute-done.12.refs_2_
  59.5 1.5 %collective-permute-start.3 = (bf16[576,128]{1,0:T(8,128)(2,1)S(1)}, bf16[576,128]{1,0:T(8,128)(2,1)S(1)}, u32[]{:S(2)}, u32[]{:S(2)}) collective-permute-start(bf16[576,128]{1,0:T(8,128)(2,1)S(1)} %get-tuple-element.28), channel_id=1, source_target_pairs={{0,1},{1,0},{2,3},{3,2},{4,5},{5,4},{6,7},{7,6},{8,9},{9,8},{10,11... | collective-permute-start | bytes 442376 | tf_op jit(solution)/shard_map/ppermute | solution.py:17
  61.0 0.0 collective-permute-done.14.refs_5_
  61.0 0.5 collective-permute-start.6
  61.5 0.0 collective-permute-done.13.refs_3_
  61.5 0.5 collective-permute-start.5
  62.0 0.0 collective-permute-done.15.refs_7_
  62.0 1.5 %collective-permute-start.7 = (bf16[576,128]{1,0:T(8,128)(2,1)S(1)}, bf16[576,128]{1,0:T(8,128)(2,1)S(1)}, u32[]{:S(2)}, u32[]{:S(2)}) collective-permute-start(bf16[576,128]{1,0:T(8,128)(2,1)S(1)} %get-tuple-element.32), channel_id=1, source_target_pairs={{0,16},{8,24},{16,0},{24,8},{1,17},{9,25},{17,1},{25,9},{2,18},{10... | collective-permute-start | bytes 442376 | tf_op jit(solution)/shard_map/ppermute | solution.py:21
  63.5 0.0 collective-permute-done.11.refs_13_
  63.5 5.2 %weight_rows.2.refs_14_ = bf16[1,3456,1280]{2,1,0:T(8,128)(2,1)} custom-call(bf16[1728,128]{1,0:T(8,128)(2,1)S(1)} %get-tuple-element.27.refs_0_, bf16[1728,128]{1,0:T(8,128)(2,1)S(1)} %collective-permute-done.2.refs_0_.refs_1_, bf16[1152,128]{1,0:T(8,128)(2,1)S(1)} %collective-permute-done.12.refs_2_, ...), custom_call_target="tpu_custom_call" | custom-call | flops 3019898880 | bytes 8257536 | tf_op jit(solution)/shard_map/weight_rows/pallas_call | solution.py:300
  68.8 0.0 collective-permute-done.3.refs_2_
  68.8 0.0 collective-permute-done.6.refs_5_
  68.8 0.0 collective-permute-done.5.refs_3_
  68.8 0.0 collective-permute-done.7.refs_7_
  68.8 3.2 %weight_rows.3 = bf16[1,3456,1280]{2,1,0:T(8,128)(2,1)} custom-call(bf16[1728,128]{1,0:T(8,128)(2,1)S(1)} %get-tuple-element.27.refs_0_, bf16[1728,128]{1,0:T(8,128)(2,1)S(1)} %collective-permute-done.2.refs_0_.refs_1_, bf16[576,128]{1,0:T(8,128)(2,1)S(1)} %collective-permute-done.3.refs_2_, ...), custom_call_target="tpu_custom_call", output_to_operand_aliasing={{}: (14, {})} | custom-call | flops 1509949440 | bytes 4128768 | tf_op jit(solution)/shard_map/weight_rows/pallas_call | solution.py:300
  (1 shorter events, 0.0 us)
Async XLA Ops:
  0.6 18.1 %collective-permute-start = (bf16[128,640]{1,0:T(8,128)(2,1)}, bf16[128,640]{1,0:T(8,128)(2,1)S(1)}, u32[]{:S(2)}, u32[]{:S(2)}) collective-permute-start(bf16[128,640]{1,0:T(8,128)(2,1)} %bitcast.3), channel_id=1, source_target_pairs={{0,4},{2,6},{4,0},{6,2},{1,5},{3,7},{5,1},{7,3},{8,12},{10,14},{12... | collective-permute-start | bytes 491528 | tf_op jit(solution)/shard_map/ppermute | solution.py:21
  4.8 0.9 %copy-start.4 = (bf16[1,1,128,640]{3,2,1,0:T(8,128)(2,1)S(1)}, bf16[1,1,128,640]{3,2,1,0:T(8,128)(2,1)}, u32[]{:S(2)}) copy-start(bf16[1,1,128,640]{3,2,1,0:T(8,128)(2,1)} %own_hbm.1) | copy-start | bytes 491524
  12.6 6.1 %copy-start = (bf16[3456,2560]{1,0:T(8,128)(2,1)}, bf16[3456,2560]{1,0:T(8,128)(2,1)S(1)}, u32[]{:S(2)}) copy-start(bf16[3456,2560]{1,0:T(8,128)(2,1)S(1)} %get-tuple-element.23.refs_1_) | copy-start | bytes 53084164
  18.7 8.3 %collective-permute-start.8 = (bf16[128,640]{1,0:T(8,128)(2,1)S(1)}, bf16[128,640]{1,0:T(8,128)(2,1)S(1)}, u32[]{:S(2)}, u32[]{:S(2)}) collective-permute-start(bf16[128,640]{1,0:T(8,128)(2,1)S(1)} %get-tuple-element.33.refs_8_), channel_id=1, source_target_pairs={{0,16},{8,24},{16,0},{24,8},{1,17},{9,25},{17,1},{25,9},{2,18},{10... | collective-permute-start | bytes 491528 | tf_op jit(solution)/shard_map/ppermute | solution.py:21
  22.0 22.8 %collective-permute-start.2 = (bf16[1728,128]{1,0:T(8,128)(2,1)S(1)}, bf16[1728,128]{1,0:T(8,128)(2,1)S(1)}, u32[]{:S(2)}, u32[]{:S(2)}) collective-permute-start(bf16[1728,128]{1,0:T(8,128)(2,1)S(1)} %get-tuple-element.27.refs_0_), channel_id=1, source_target_pairs={{0,16},{8,24},{16,0},{24,8},{1,17},{9,25},{17,1},{25,9},{2,18},{10... | collective-permute-start | bytes 1327112 | tf_op jit(solution)/shard_map/ppermute | solution.py:21
  22.5 22.7 %collective-permute-start.4 = (bf16[1728,128]{1,0:T(8,128)(2,1)S(1)}, bf16[1728,128]{1,0:T(8,128)(2,1)S(1)}, u32[]{:S(2)}, u32[]{:S(2)}) collective-permute-start(bf16[1728,128]{1,0:T(8,128)(2,1)S(1)} %get-tuple-element.29.refs_4_), channel_id=1, source_target_pairs={{0,1},{1,0},{2,3},{3,2},{4,5},{5,4},{6,7},{7,6},{8,9},{9,8},{10,11... | collective-permute-start | bytes 1327112 | tf_op jit(solution)/shard_map/ppermute | solution.py:17
  24.0 14.8 %collective-permute-start.9 = (bf16[128,640]{1,0:T(8,128)(2,1)S(1)}, bf16[128,640]{1,0:T(8,128)(2,1)S(1)}, u32[]{:S(2)}, u32[]{:S(2)}) collective-permute-start(bf16[128,640]{1,0:T(8,128)(2,1)S(1)} %get-tuple-element.34), channel_id=1, source_target_pairs={{0,1},{1,0},{2,3},{3,2},{4,5},{5,4},{6,7},{7,6},{8,9},{9,8},{10,11... | collective-permute-start | bytes 491528 | tf_op jit(solution)/shard_map/ppermute | solution.py:17
  24.6 17.0 %collective-permute-start.10 = (bf16[128,640]{1,0:T(8,128)(2,1)S(1)}, bf16[128,640]{1,0:T(8,128)(2,1)S(1)}, u32[]{:S(2)}, u32[]{:S(2)}) collective-permute-start(bf16[128,640]{1,0:T(8,128)(2,1)S(1)} %get-tuple-element.34), channel_id=1, source_target_pairs={{0,17},{1,16},{8,25},{9,24},{16,1},{17,0},{24,9},{25,8},{2,19},{3,... | collective-permute-start | bytes 491528 | tf_op jit(solution)/shard_map/ppermute | solution.py:31
  27.0 18.9 %collective-permute-start.1 = (bf16[2,128,640]{2,1,0:T(8,128)(2,1)S(1)}, bf16[2,128,640]{2,1,0:T(8,128)(2,1)S(1)}, u32[]{:S(2)}, u32[]{:S(2)}) collective-permute-start(bf16[2,128,640]{2,1,0:T(8,128)(2,1)S(1)} %get-tuple-element.22), channel_id=1, source_target_pairs={{0,2},{2,0},{4,6},{6,4},{1,3},{3,1},{5,7},{7,5},{8,10},{10,8},{12,... | collective-permute-start | bytes 983048 | tf_op jit(solution)/shard_map/ppermute | solution.py:21
  41.6 21.9 %collective-permute-start.11 = (bf16[3,128,640]{2,1,0:T(8,128)(2,1)S(1)}, bf16[3,128,640]{2,1,0:T(8,128)(2,1)S(1)}, u32[]{:S(2)}, u32[]{:S(2)}) collective-permute-start(bf16[3,128,640]{2,1,0:T(8,128)(2,1)S(1)} %shard_map.69), channel_id=1, source_target_pairs={{0,2},{2,0},{4,6},{6,4},{1,3},{3,1},{5,7},{7,5},{8,10},{10,8},{12,... | collective-permute-start | bytes 1474568 | tf_op jit(solution)/shard_map/ppermute | solution.py:21
  43.3 16.2 %collective-permute-start.12 = (bf16[1152,128]{1,0:T(8,128)(2,1)S(1)}, bf16[1152,128]{1,0:T(8,128)(2,1)S(1)}, u32[]{:S(2)}, u32[]{:S(2)}) collective-permute-start(bf16[1152,128]{1,0:T(8,128)(2,1)S(1)} %get-tuple-element.35), channel_id=1, source_target_pairs={{0,1},{1,0},{2,3},{3,2},{4,5},{5,4},{6,7},{7,6},{8,9},{9,8},{10,11... | collective-permute-start | bytes 884744 | tf_op jit(solution)/shard_map/ppermute | solution.py:17
  44.8 16.2 %collective-permute-start.14 = (bf16[1152,128]{1,0:T(8,128)(2,1)S(1)}, bf16[1152,128]{1,0:T(8,128)(2,1)S(1)}, u32[]{:S(2)}, u32[]{:S(2)}) collective-permute-start(bf16[1152,128]{1,0:T(8,128)(2,1)S(1)} %get-tuple-element.37), channel_id=1, source_target_pairs={{0,16},{8,24},{16,0},{24,8},{1,17},{9,25},{17,1},{25,9},{2,18},{10... | collective-permute-start | bytes 884744 | tf_op jit(solution)/shard_map/ppermute | solution.py:21
  45.3 16.1 %collective-permute-start.13 = (bf16[1152,128]{1,0:T(8,128)(2,1)S(1)}, bf16[1152,128]{1,0:T(8,128)(2,1)S(1)}, u32[]{:S(2)}, u32[]{:S(2)}) collective-permute-start(bf16[1152,128]{1,0:T(8,128)(2,1)S(1)} %get-tuple-element.36), channel_id=1, source_target_pairs={{0,1},{1,0},{2,3},{3,2},{4,5},{5,4},{6,7},{7,6},{8,9},{9,8},{10,11... | collective-permute-start | bytes 884744 | tf_op jit(solution)/shard_map/ppermute | solution.py:17
  45.9 16.1 %collective-permute-start.15 = (bf16[1152,128]{1,0:T(8,128)(2,1)S(1)}, bf16[1152,128]{1,0:T(8,128)(2,1)S(1)}, u32[]{:S(2)}, u32[]{:S(2)}) collective-permute-start(bf16[1152,128]{1,0:T(8,128)(2,1)S(1)} %get-tuple-element.38), channel_id=1, source_target_pairs={{0,16},{8,24},{16,0},{24,8},{1,17},{9,25},{17,1},{25,9},{2,18},{10... | collective-permute-start | bytes 884744 | tf_op jit(solution)/shard_map/ppermute | solution.py:21
  47.5 6.0 %copy-start.1 = (bf16[3456,2560]{1,0:T(8,128)(2,1)S(1)}, bf16[3456,2560]{1,0:T(8,128)(2,1)}, u32[]{:S(2)}) copy-start(bf16[3456,2560]{1,0:T(8,128)(2,1)} %copy-done) | copy-start | bytes 53084164
  53.5 2.0 %copy-start.2 = (bf16[1,1,3456,128]{3,2,1,0:T(8,128)(2,1)S(1)}, bf16[1,1,3456,128]{3,2,1,0:T(8,128)(2,1)}, u32[]{:S(2)}) copy-start(bf16[1,1,3456,128]{3,2,1,0:T(8,128)(2,1)} %gate_hbm.1) | copy-start | bytes 2654212
  53.5 2.0 %copy-start.3 = (bf16[1,1,3456,128]{3,2,1,0:T(8,128)(2,1)S(1)}, bf16[1,1,3456,128]{3,2,1,0:T(8,128)(2,1)}, u32[]{:S(2)}) copy-start(bf16[1,1,3456,128]{3,2,1,0:T(8,128)(2,1)} %up_hbm.1) | copy-start | bytes 2654212
  59.5 9.3 %collective-permute-start.3 = (bf16[576,128]{1,0:T(8,128)(2,1)S(1)}, bf16[576,128]{1,0:T(8,128)(2,1)S(1)}, u32[]{:S(2)}, u32[]{:S(2)}) collective-permute-start(bf16[576,128]{1,0:T(8,128)(2,1)S(1)} %get-tuple-element.28), channel_id=1, source_target_pairs={{0,1},{1,0},{2,3},{3,2},{4,5},{5,4},{6,7},{7,6},{8,9},{9,8},{10,11... | collective-permute-start | bytes 442376 | tf_op jit(solution)/shard_map/ppermute | solution.py:17
  61.0 7.8 %collective-permute-start.6 = (bf16[576,128]{1,0:T(8,128)(2,1)S(1)}, bf16[576,128]{1,0:T(8,128)(2,1)S(1)}, u32[]{:S(2)}, u32[]{:S(2)}) collective-permute-start(bf16[576,128]{1,0:T(8,128)(2,1)S(1)} %get-tuple-element.31), channel_id=1, source_target_pairs={{0,16},{8,24},{16,0},{24,8},{1,17},{9,25},{17,1},{25,9},{2,18},{10... | collective-permute-start | bytes 442376 | tf_op jit(solution)/shard_map/ppermute | solution.py:21
  61.5 7.3 %collective-permute-start.5 = (bf16[576,128]{1,0:T(8,128)(2,1)S(1)}, bf16[576,128]{1,0:T(8,128)(2,1)S(1)}, u32[]{:S(2)}, u32[]{:S(2)}) collective-permute-start(bf16[576,128]{1,0:T(8,128)(2,1)S(1)} %get-tuple-element.30), channel_id=1, source_target_pairs={{0,1},{1,0},{2,3},{3,2},{4,5},{5,4},{6,7},{7,6},{8,9},{9,8},{10,11... | collective-permute-start | bytes 442376 | tf_op jit(solution)/shard_map/ppermute | solution.py:17
  62.0 6.8 %collective-permute-start.7 = (bf16[576,128]{1,0:T(8,128)(2,1)S(1)}, bf16[576,128]{1,0:T(8,128)(2,1)S(1)}, u32[]{:S(2)}, u32[]{:S(2)}) collective-permute-start(bf16[576,128]{1,0:T(8,128)(2,1)S(1)} %get-tuple-element.32), channel_id=1, source_target_pairs={{0,16},{8,24},{16,0},{24,8},{1,17},{9,25},{17,1},{25,9},{2,18},{10... | collective-permute-start | bytes 442376 | tf_op jit(solution)/shard_map/ppermute | solution.py:21
